TPU v7x, 128 devices: a whole 4x4x4 slice. The times are simulated.
128 devices in a mesh: row: 16 (over x, z), col: 8 (over y, core).
Axes of the slice: x: 4, y: 4, z: 4, core: 2. Of those that a mesh axis runs over, the one named last changes fastest.
Arguments:
- blocks: bfloat16 [512, 16, 128, 128], P('row', 'col'), may hold values from -0.375 to 0.375
- pattern: int32 [512, 16], replicated, may hold values from 0 to 511, as said below
- owners: int32 [8, 512, 2, 1], P('col', 'row'), may hold values from 0 to 15; in each aligned block of 64 rows (0 to 63, 64 to 127, ..., all dimensions but the last counted through in order) at most 6 rows name the same one
Outputs:
- moved: bfloat16 [8, 16, 96, 128, 128], P('col', 'row')
Inputs may be any that keep to these rules, and one draw needn't show every extreme that they name: `pattern`: block row i holds 16 distinct column blocks (i + d) mod 512, by rising d with |d| <= 8, d = 0 among them, in slot order. `owners`: among the 64 entries of one device no value occurs more than 6 times; in some device some value occurs exactly 6 times.
All inputs are finite; a program needn't handle non-finite values.
Results may differ from a plain program's by a relative error of at most 0.0049.
Values may be sent and summed in bfloat16 or wider, within the bound.
No kernel may reach another device: no remote copies, remote signals or barrier semaphores. Data moves between devices by JAX's collectives and lax.ppermute only.
A program may use at most 192 MiB of HBM per device.

v0:
```python
import math
import jax
import jax.numpy as jnp
from jax import lax
from jax.sharding import PartitionSpec as P


def extended_2(shard, sides, width):
    for axis, dim in sides:
        devices, length = (lax.axis_size(axis), shard.shape[dim])
        up = [(i, (i + 1) % devices) for i in range(devices)]
        down = [(j, i) for i, j in up]
        last = lax.slice_in_dim(shard, length - width, length, axis=dim)
        first = lax.slice_in_dim(shard, 0, width, axis=dim)
        before = lax.ppermute(last, axis, up)
        after = lax.ppermute(first, axis, down)
        shard = jnp.concatenate([before, shard, after], axis=dim)
    return shard


def local_index(pattern, start_row, row_count, margin, slot_start, target_count):
    nblk, slot_count = pattern.shape
    reach = slot_count // 2
    own_cols = lax.dynamic_slice_in_dim(pattern, start_row, row_count, 0)
    row_ids = start_row + jnp.arange(row_count, dtype=jnp.int32)
    offsets = (own_cols - row_ids[:, None] + reach + nblk) % nblk - reach
    ext_row = jnp.arange(row_count, dtype=jnp.int32)[:, None] + margin + offsets
    neighbour_cols = pattern[own_cols]
    wanted = lax.dynamic_slice_in_dim(own_cols, slot_start, target_count, 1)
    same_col = neighbour_cols[:, None, :, :] == wanted[:, :, None, None]
    has_match = jnp.any(same_col, axis=-1)
    match_slot = jnp.sum(
        same_col.astype(jnp.int32) * jnp.arange(slot_count, dtype=jnp.int32), axis=-1
    )
    extent = (row_count + 2 * margin) * slot_count
    return jnp.where(has_match, ext_row[:, None, :] * slot_count + match_slot, extent)


def multiply(left, extended, pick_index):
    row_count, slot_count, tile_size = (left.shape[0], left.shape[1], left.shape[-1])
    target_count = pick_index.shape[1]
    group_rows = math.gcd(row_count, max(1, 32 // target_count))
    flat_table = jnp.concatenate(
        [
            extended.reshape(-1, tile_size, tile_size),
            jnp.zeros((1, tile_size, tile_size), extended.dtype),
        ],
        axis=0,
    )

    def per_group(operands):
        left_rows, pick_rows = operands
        picked = flat_table[pick_rows]
        return jnp.einsum("gtab,gstbc->gsac", left_rows, picked, preferred_element_type=jnp.float32)

    result = lax.map(
        per_group,
        (
            left.reshape(row_count // group_rows, group_rows, slot_count, tile_size, tile_size),
            pick_index.reshape(row_count // group_rows, group_rows, target_count, slot_count),
        ),
    )
    return result.reshape(row_count, target_count, tile_size, tile_size)


def per_device(blocks, pattern, owners):
    row_count, slot_share, tile_size = (blocks.shape[0], blocks.shape[1], blocks.shape[-1])
    slot_count = pattern.shape[1]
    reach = slot_count // 2
    row_pos = lax.axis_index("row")
    col_pos = lax.axis_index("col")
    row_devices = lax.axis_size("row")
    full_rows = lax.all_gather(blocks, "col", axis=1, tiled=True)
    extended = extended_2(full_rows, (("row", 0),), reach)
    pick_index = local_index(
        pattern, row_pos * row_count, row_count, reach, col_pos * slot_share, slot_share
    )
    squared = multiply(full_rows, extended, pick_index).astype(jnp.bfloat16)
    square_rows = lax.all_gather(squared, "col", axis=1, tiled=True)
    cube_term = multiply(square_rows, extended, pick_index)
    result = (3.0 * squared.astype(jnp.float32) - 2.0 * cube_term).astype(jnp.bfloat16)
    block_count = row_count * slot_share
    capacity = 3 * block_count // (2 * row_devices)
    flat_result = result.reshape(block_count, tile_size, tile_size)
    destination = owners.reshape(block_count)
    one_hot = (destination[:, None] == jnp.arange(row_devices, dtype=jnp.int32)[None, :]).astype(
        jnp.int32
    )
    bucket_rank = jnp.sum((jnp.cumsum(one_hot, axis=0) - 1) * one_hot, axis=1)
    bucket_slot = destination * capacity + bucket_rank
    wanted = jnp.arange(row_devices * capacity, dtype=jnp.int32)
    slot_match = bucket_slot[None, :] == wanted[:, None]
    has_source = jnp.any(slot_match, axis=1)
    source = jnp.sum(
        slot_match.astype(jnp.int32) * jnp.arange(block_count, dtype=jnp.int32)[None, :], axis=1
    )
    padded = jnp.concatenate(
        [flat_result, jnp.zeros((1, tile_size, tile_size), flat_result.dtype)], axis=0
    )
    buckets = padded[jnp.where(has_source, source, block_count)].reshape(
        row_devices, capacity, tile_size, tile_size
    )
    received = lax.all_to_all(buckets, "row", split_axis=0, concat_axis=0, tiled=True)
    return received.reshape(1, 1, row_devices * capacity, tile_size, tile_size)


def solution(mesh):
    in_specs = (P("row", "col", None, None), P(), P("col", "row", None, None))
    out_specs = P("col", "row", None, None, None)
    return jax.shard_map(
        per_device, mesh=mesh, in_specs=in_specs, out_specs=out_specs, check_vma=False
    )
```

profile of v0, /device:TPU:8, one launch (start us, length us, event | category | flops | bytes accessed | tf_op | source)
XLA Modules:
  0.0 546.1 jit_solution(1662284565458652383)
XLA Ops:
  7.3 88.5 %all-gather.3.cloned.1.call-done = bf16[32,16,128,128]{3,2,1,0:T(8,128)(2,1)} async-done(((bf16[32,2,128,128]{3,2,1,0:T(8,128)(2,1)}), bf16[32,16,128,128]{3,2,1,0:T(8,128)(2,1)}) %all-gather.3.cloned.1.call-update) | async-done | bytes 16777232 | tf_op jit(solution)/shard_map/all_gather | solution.py:73
  95.9 6.0 %fusion.20 = (bf16[8,16,128,128]{3,2,1,0:T(8,128)(2,1)}, bf16[8,16,128,128]{3,2,1,0:T(8,128)(2,1)}) fusion(bf16[32,16,128,128]{3,2,1,0:T(8,128)(2,1)} %all-gather.3.cloned.1.call-done), kind=kLoop, calls=%fused_computation.45 | loop fusion | bytes 16777216 | tf_op jit(solution)/shard_map/slice | solution.py:13
  101.9 1.6 collective-permute-start
  103.4 3.8 collective-permute-start.1
  109.9 88.4 %collective-permute-done = bf16[8,16,128,128]{3,2,1,0:T(8,128)(2,1)} collective-permute-done((bf16[8,16,128,128]{3,2,1,0:T(8,128)(2,1)}, bf16[8,16,128,128]{3,2,1,0:T(8,128)(2,1)}, u32[]{:S(2)}, u32[]{:S(2)}) %collective-permute-start) | collective-permute-done | bytes 4194336 | tf_op jit(solution)/shard_map/ppermute | solution.py:15
  198.3 17.7 %pad_maximum_fusion = bf16[48,16,128,128]{3,2,1,0:T(8,128)(2,1)} fusion(bf16[8,16,128,128]{3,2,1,0:T(8,128)(2,1)} %collective-permute-done.1, bf16[32,16,128,128]{3,2,1,0:T(8,128)(2,1)} %all-gather.3.cloned.1.call-done, bf16[8,16,128,128]{3,2,1,0:T(8,128)(2,1)} %collective-permute-done), kind=kLoop, calls=%fused_computation.18 | loop fusion | flops 25165824 | bytes 50331648 | tf_op jit(solution)/shard_map/concatenate | solution.py:17
  216.0 22.0 %concatenate.11 = bf16[769,128,128]{2,1,0:T(8,128)(2,1)} pad(bf16[768,128,128]{2,1,0:T(8,128)(2,1)} %bitcast.93, bf16[]{:T(256)} %constant.99.clone.1), padding=0_1x0_0x0_0 | pad | bytes 50364416 | tf_op jit(solution)/shard_map/concatenate | solution.py:43
  237.9 66.3 %while.22 = (s32[]{:T(128)}, bf16[2,16,2,128,128]{3,4,2,1,0:T(8,128)(2,1)S(1)}, s32[2,16,2,16]{3,2,1,0:T(2,128)S(1)}, bf16[769,128,128]{2,1,0:T(8,128)(2,1)}, bf16[2,16,16,128,128]{4,3,2,1,0:T(8,128)(2,1)}) while((s32[]{:T(128)}, bf16[2,16,2,128,128]{3,4,2,1,0:T(8,128)(2,1)S(1)}, s32[2,16,2,16]{3,2,1,0:T(2,128)S(1)}, ...), condition=%wide.region_3.4_spmd.clone, body=%wide.region_2.3_spmd.sunk.clone | while | flops 2147486208 | bytes 60834880 | solution.py:56
  238.1 21.9 %gather_fusion = bf16[512,128,128]{2,1,0:T(8,128)(2,1)} fusion(bf16[769,128,128]{2,1,0:T(8,128)(2,1)} %get-tuple-element.196, s32[1024]{0:T(1024)S(1)} %pad_clamp_fusion.8), kind=kCustom, calls=%fused_computation.clone.1.clone | custom fusion | bytes 33556480 | tf_op jit(solution)/shard_map/while/body/eval_jaxpr/gather | solution.py:53
  259.9 11.2 %bitcast_dynamic-update-slice_fusion.6 = bf16[2,16,2,128,128]{3,4,2,1,0:T(8,128)(2,1)S(1)} fusion(bf16[2,16,2,128,128]{3,4,2,1,0:T(8,128)(2,1)S(1)} %get-tuple-element.189, s32[]{:T(128)} %get-tuple-element.188, bf16[16,2,16,128,128]{4,3,2,1,0:T(8,128)(2,1)} %bitcast.91, bf16[2,16,16,128,128]{4,3,2,1,0:T(8,128)(2,1)} %get-tuple-element.197), kind=kOutput, calls=%fused_computation.7.clone.1.clone | convolution fusion | flops 2147483648 | bytes 27264000 | tf_op jit(solution)/shard_map/while/body/eval_jaxpr/gtab,gstbc->gsac/dot_general | solution.py:54
  271.2 21.9 %gather_fusion = bf16[512,128,128]{2,1,0:T(8,128)(2,1)} fusion(bf16[769,128,128]{2,1,0:T(8,128)(2,1)} %get-tuple-element.196, s32[1024]{0:T(1024)S(1)} %pad_clamp_fusion.8), kind=kCustom, calls=%fused_computation.clone.1.clone | custom fusion | bytes 33556480 | tf_op jit(solution)/shard_map/while/body/eval_jaxpr/gather | solution.py:53
  293.1 11.2 %bitcast_dynamic-update-slice_fusion.6 = bf16[2,16,2,128,128]{3,4,2,1,0:T(8,128)(2,1)S(1)} fusion(bf16[2,16,2,128,128]{3,4,2,1,0:T(8,128)(2,1)S(1)} %get-tuple-element.189, s32[]{:T(128)} %get-tuple-element.188, bf16[16,2,16,128,128]{4,3,2,1,0:T(8,128)(2,1)} %bitcast.91, bf16[2,16,16,128,128]{4,3,2,1,0:T(8,128)(2,1)} %get-tuple-element.197), kind=kOutput, calls=%fused_computation.7.clone.1.clone | convolution fusion | flops 2147483648 | bytes 27264000 | tf_op jit(solution)/shard_map/while/body/eval_jaxpr/gtab,gstbc->gsac/dot_general | solution.py:54
  306.4 84.6 %all-gather.5.cloned.1.call-done = bf16[32,16,128,128]{2,3,1,0:T(8,128)(2,1)} async-done(((bf16[32,2,128,128]{2,3,1,0:T(8,128)(2,1)}), bf16[32,16,128,128]{2,3,1,0:T(8,128)(2,1)}) %all-gather.5.cloned.1.call-update) | async-done | bytes 16777232 | tf_op jit(solution)/shard_map/all_gather | solution.py:79
  391.1 22.5 %copy.41 = bf16[32,16,128,128]{3,2,1,0:T(8,128)(2,1)} copy(bf16[32,16,128,128]{2,3,1,0:T(8,128)(2,1)} %all-gather.5.cloned.1.call-done) | data formatting | bytes 33554432 | tf_op jit(solution)/shard_map/all_gather | solution.py:79
  413.6 67.6 %while.23 = (s32[]{:T(128)}, f32[2,16,2,128,128]{3,4,2,1,0:T(8,128)}, s32[2,16,2,16]{3,2,1,0:T(2,128)S(1)}, bf16[769,128,128]{2,1,0:T(8,128)(2,1)}, bf16[2,16,16,128,128]{4,3,2,1,0:T(8,128)(2,1)}) while((s32[]{:T(128)}, f32[2,16,2,128,128]{3,4,2,1,0:T(8,128)}, s32[2,16,2,16]{3,2,1,0:T(2,128)S(1)}, ...), condition=%wide.region_5.6_spmd.clone, body=%wide.region_4.5_spmd.sunk.clone | while | flops 2147486208 | bytes 60834880 | solution.py:56
  413.7 22.0 %gather_fusion.1 = bf16[512,128,128]{2,1,0:T(8,128)(2,1)} fusion(bf16[769,128,128]{2,1,0:T(8,128)(2,1)} %get-tuple-element.211, s32[1024]{0:T(1024)S(1)} %pad_clamp_fusion.9), kind=kCustom, calls=%fused_computation.1.clone.1.clone | custom fusion | bytes 33556480 | tf_op jit(solution)/shard_map/while/body/eval_jaxpr/gather | solution.py:53
  435.7 11.7 %bitcast_dynamic-update-slice_fusion.7 = f32[2,16,2,128,128]{3,4,2,1,0:T(8,128)} fusion(f32[2,16,2,128,128]{3,4,2,1,0:T(8,128)} %get-tuple-element.204, s32[]{:T(128)} %get-tuple-element.203, bf16[16,2,16,128,128]{4,3,2,1,0:T(8,128)(2,1)} %bitcast.92, bf16[2,16,16,128,128]{4,3,2,1,0:T(8,128)(2,1)} %get-tuple-element.212), kind=kOutput, calls=%fused_computation.14.clone.1.clone | convolution fusion | flops 2147483648 | bytes 27264000 | tf_op jit(solution)/shard_map/while/body/eval_jaxpr/gtab,gstbc->gsac/dot_general | solution.py:54
  447.5 21.9 %gather_fusion.1 = bf16[512,128,128]{2,1,0:T(8,128)(2,1)} fusion(bf16[769,128,128]{2,1,0:T(8,128)(2,1)} %get-tuple-element.211, s32[1024]{0:T(1024)S(1)} %pad_clamp_fusion.9), kind=kCustom, calls=%fused_computation.1.clone.1.clone | custom fusion | bytes 33556480 | tf_op jit(solution)/shard_map/while/body/eval_jaxpr/gather | solution.py:53
  469.4 11.8 %bitcast_dynamic-update-slice_fusion.7 = f32[2,16,2,128,128]{3,4,2,1,0:T(8,128)} fusion(f32[2,16,2,128,128]{3,4,2,1,0:T(8,128)} %get-tuple-element.204, s32[]{:T(128)} %get-tuple-element.203, bf16[16,2,16,128,128]{4,3,2,1,0:T(8,128)(2,1)} %bitcast.92, bf16[2,16,16,128,128]{4,3,2,1,0:T(8,128)(2,1)} %get-tuple-element.212), kind=kOutput, calls=%fused_computation.14.clone.1.clone | convolution fusion | flops 2147483648 | bytes 27264000 | tf_op jit(solution)/shard_map/while/body/eval_jaxpr/gtab,gstbc->gsac/dot_general | solution.py:54
  481.2 2.9 subtract_convert_fusion
  484.3 2.7 gather_fusion.3
  487.0 3.5 copy.44
  490.5 47.1 %all_to_all.5 = bf16[16,6,128,128]{3,2,1,0:T(8,128)(2,1)S(1)} all-to-all(bf16[16,6,128,128]{3,2,1,0:T(8,128)(2,1)S(1)} %bitcast.97), channel_id=1, replica_groups=mesh['row'=16,'col'=8] {'row'}, dimensions={0} | all-to-all | bytes 6291456 | tf_op jit(solution)/shard_map/all_to_all | solution.py:103
  537.6 1.7 copy.69
  (54 shorter events, 6.0 us)
Async XLA Ops:
  6.5 89.3 %all-gather.3.cloned.1.call-start = ((), (), s32[]{:S(2)}) async-start(), calls=%async_computation.1 | async-start | bytes 18874368 | tf_op jit(solution)/shard_map/all_gather | solution.py:73
  7.3 100.0 %copy-start.2 = (s32[512,16]{0,1:T(8,128)S(1)}, s32[512,16]{0,1:T(8,128)}, u32[]{:S(2)}) copy-start(s32[512,16]{0,1:T(8,128)} %param.8) | copy-start | bytes 98308
  7.3 383.8 %all-gather.5.cloned.1.call-start = ((), (), s32[]{:S(2)}) async-start(), calls=%async_computation.2 | async-start | bytes 18874368 | tf_op jit(solution)/shard_map/all_gather | solution.py:79
  101.9 96.4 %collective-permute-start = (bf16[8,16,128,128]{3,2,1,0:T(8,128)(2,1)}, bf16[8,16,128,128]{3,2,1,0:T(8,128)(2,1)}, u32[]{:S(2)}, u32[]{:S(2)}) collective-permute-start(bf16[8,16,128,128]{3,2,1,0:T(8,128)(2,1)} %get-tuple-element.91), channel_id=1, source_target_pairs={{0,8},{8,16},{16,24},{24,32},{32,40},{40,48},{48,56},{56,64},{64,7... | collective-permute-start | bytes 12582920 | tf_op jit(solution)/shard_map/ppermute | solution.py:15
  103.4 94.8 %collective-permute-start.1 = (bf16[8,16,128,128]{3,2,1,0:T(8,128)(2,1)}, bf16[8,16,128,128]{3,2,1,0:T(8,128)(2,1)}, u32[]{:S(2)}, u32[]{:S(2)}) collective-permute-start(bf16[8,16,128,128]{3,2,1,0:T(8,128)(2,1)} %get-tuple-element.92), channel_id=1, source_target_pairs={{8,0},{16,8},{24,16},{32,24},{40,32},{48,40},{56,48},{64,56},{72,6... | collective-permute-start | bytes 12582920 | tf_op jit(solution)/shard_map/ppermute | solution.py:16
  237.9 67.7 %copy-start.3 = (s32[1,32,2,1]{1,3,2,0:T(1,128)S(1)}, s32[1,32,2,1]{1,3,2,0:T(1,128)}, u32[]{:S(2)}) copy-start(s32[1,32,2,1]{1,3,2,0:T(1,128)} %param.9) | copy-start | bytes 772
  304.3 1.3 copy-start
  413.6 67.6 %copy-start.1 = (bf16[2,16,2,128,128]{3,4,2,1,0:T(8,128)(2,1)S(1)}, bf16[2,16,2,128,128]{3,4,2,1,0:T(8,128)(2,1)}, u32[]{:S(2)}) copy-start(bf16[2,16,2,128,128]{3,4,2,1,0:T(8,128)(2,1)} %copy-done) | copy-start | bytes 6291460
Sparse Core Ops, SparseCore 0:
  9.0 86.7 all-gather.2
  305.8 85.2 all-gather.4
where the time goes:
time: 547 us; the launch traced here: 546 us
  waiting for transfers between devices  262 us (48%)
  local copies, waits for them, and re-layouts  150 us (27%)
  blocking collectives  47.1 us (9%)
  matrix products  45.9 us (8%)
  other arithmetic  22 us (4%)
  between operations  13.6 us (2%)
    all_gather x1, waiting for transfers between devices, per_device(): full_rows = lax.all_gather(blocks, 'col', axis=1, tiled=True)  88.5 us
    ppermute x1, waiting for transfers between devices, extended_2(): before = lax.ppermute(last, axis, up)  88.4 us
    gather x4, local copies, waits for them, and re-layouts, per_group(): picked = flat_table[pick_rows]  87.6 us
    all_gather x1, waiting for transfers between devices, per_device(): square_rows = lax.all_gather(squared, 'col', axis=1, tiled=True)  84.6 us
    all_to_all x1, blocking collectives, per_device(): lax.all_to_all(buckets, 'row', split_axis=0, concat_axis=0, tiled=True)  47.1 us
    dot_general x4, matrix products, per_group(): jnp.einsum('gtab,gstbc->gsac', left_rows, picked, preferred_element_type=...  45.9 us
    all_gather x1, local copies, waits for them, and re-layouts, per_device(): square_rows = lax.all_gather(squared, 'col', axis=1, tiled=True)  22.5 us
    concatenate x1, local copies, waits for them, and re-layouts, multiply(): jnp.concatenate([extended.reshape(-1, tile_size, tile_size), jnp.zeros((1...  22 us
  transfers between devices with their start and end apart: 4, of which 3 were waited for; matrix products, arithmetic and copies ran while one was open for 1% of the time, Pallas kernels for 0%

commit v1 on v0

--- a/solution.py
+++ b/solution.py
@@ -70,7 +70,9 @@
     row_pos = lax.axis_index("row")
     col_pos = lax.axis_index("col")
     row_devices = lax.axis_size("row")
-    full_rows = lax.all_gather(blocks, "col", axis=1, tiled=True)
+    full_rows = jnp.concatenate(
+        lax.all_to_all(jnp.stack([blocks] * lax.axis_size("col")), "col", 0, 0), axis=1
+    )
     extended = extended_2(full_rows, (("row", 0),), reach)
     pick_index = local_index(
         pattern, row_pos * row_count, row_count, reach, col_pos * slot_share, slot_share

time: 547 us -> 657 us (1.20)
  blocking collectives: 47.1 us -> 237 us
  waiting for transfers between devices: 262 us -> 172 us
  local copies, waits for them, and re-layouts: 150 us -> 159 us
    all_to_all x0 -> x1, blocking collectives: none -> 190 us  [per_device(): lax.all_to_all(jnp.stack([blocks] * lax.axis_size('col')), 'col', 0, 0)]
    all_gather x1 -> x0, waiting for transfers between devices: 88.5 us -> none  [per_device(): full_rows = lax.all_gather(blocks, 'col', axis=1, tiled=True)]
  transfers between devices with their start and end apart: 4 -> 3, of which waited for: 3 -> 2; matrix products, arithmetic and copies ran while one was open for 1% -> 1% of each run, Pallas kernels for 0% -> 0%
where the time goes in v1:
time: 657 us; the launch traced here: 656 us
  blocking collectives  237 us (36%)
  waiting for transfers between devices  172 us (26%)
  local copies, waits for them, and re-layouts  159 us (24%)
  matrix products  45.9 us (7%)
  other arithmetic  22 us (3%)
  between operations  13.6 us (2%)
    all_to_all x1, blocking collectives, per_device(): lax.all_to_all(jnp.stack([blocks] * lax.axis_size('col')), 'col', 0, 0)  190 us
    ppermute x1, waiting for transfers between devices, extended_2(): before = lax.ppermute(last, axis, up)  87.9 us
    gather x4, local copies, waits for them, and re-layouts, per_group(): picked = flat_table[pick_rows]  87.6 us
    all_gather x1, waiting for transfers between devices, per_device(): square_rows = lax.all_gather(squared, 'col', axis=1, tiled=True)  84.1 us
    all_to_all x1, blocking collectives, per_device(): lax.all_to_all(buckets, 'row', split_axis=0, concat_axis=0, tiled=True)  47.1 us
    dot_general x4, matrix products, per_group(): jnp.einsum('gtab,gstbc->gsac', left_rows, picked, preferred_element_type=...  45.9 us
    all_gather x1, local copies, waits for them, and re-layouts, per_device(): square_rows = lax.all_gather(squared, 'col', axis=1, tiled=True)  22.5 us
    concatenate x1, local copies, waits for them, and re-layouts, multiply(): jnp.concatenate([extended.reshape(-1, tile_size, tile_size), jnp.zeros((1...  22 us
  transfers between devices with their start and end apart: 3, of which 2 were waited for; matrix products, arithmetic and copies ran while one was open for 1% of the time, Pallas kernels for 0%

profile of v1, /device:TPU:8, one launch (start us, length us, event | category | flops | bytes accessed | tf_op | source)
XLA Modules:
  0.0 656.2 jit_solution(3914525302599215496)
XLA Ops:
  6.5 5.1 stack.2
  11.7 190.1 %all_to_all.10 = bf16[8,32,2,128,128]{4,3,2,1,0:T(8,128)(2,1)S(1)} all-to-all(bf16[8,32,2,128,128]{4,3,2,1,0:T(8,128)(2,1)S(1)} %stack.2), channel_id=1, replica_groups=mesh['row'=16,'col'=8] {'col'}, dimensions={0} | all-to-all | bytes 33554432 | tf_op jit(solution)/shard_map/all_to_all | solution.py:74
  204.0 4.1 fusion.20
  208.0 4.1 copy-done
  214.1 4.3 collective-permute-start.1
  221.0 87.9 %collective-permute-done = bf16[8,16,128,128]{3,2,1,0:T(8,128)(2,1)} collective-permute-done((bf16[8,16,128,128]{3,2,1,0:T(8,128)(2,1)}, bf16[8,16,128,128]{3,2,1,0:T(8,128)(2,1)}, u32[]{:S(2)}, u32[]{:S(2)}) %collective-permute-start) | collective-permute-done | bytes 4194336 | tf_op jit(solution)/shard_map/ppermute | solution.py:15
  308.9 17.7 %pad_maximum_fusion = bf16[48,16,128,128]{3,2,1,0:T(8,128)(2,1)} fusion(bf16[8,16,128,128]{3,2,1,0:T(8,128)(2,1)} %collective-permute-done.1, bf16[32,16,128,128]{3,2,1,0:T(8,128)(2,1)} %bitcast.101, bf16[8,16,128,128]{3,2,1,0:T(8,128)(2,1)} %collective-permute-done), kind=kLoop, calls=%fused_computation.18 | loop fusion | flops 25165824 | bytes 50331648 | tf_op jit(solution)/shard_map/concatenate | solution.py:17
  326.6 22.0 %concatenate.11 = bf16[769,128,128]{2,1,0:T(8,128)(2,1)} pad(bf16[768,128,128]{2,1,0:T(8,128)(2,1)} %bitcast.103, bf16[]{:T(256)} %constant.99.clone.1), padding=0_1x0_0x0_0 | pad | bytes 50364416 | tf_op jit(solution)/shard_map/concatenate | solution.py:43
  348.6 66.3 %while.22 = (s32[]{:T(128)}, bf16[2,16,2,128,128]{3,4,2,1,0:T(8,128)(2,1)S(1)}, s32[2,16,2,16]{3,2,1,0:T(2,128)S(1)}, bf16[769,128,128]{2,1,0:T(8,128)(2,1)}, bf16[2,16,16,128,128]{4,3,2,1,0:T(8,128)(2,1)}) while((s32[]{:T(128)}, bf16[2,16,2,128,128]{3,4,2,1,0:T(8,128)(2,1)S(1)}, s32[2,16,2,16]{3,2,1,0:T(2,128)S(1)}, ...), condition=%wide.region_3.4_spmd.clone, body=%wide.region_2.3_spmd.sunk.clone | while | flops 2147486208 | bytes 60834880 | solution.py:56
  348.7 21.9 %gather_fusion = bf16[512,128,128]{2,1,0:T(8,128)(2,1)} fusion(bf16[769,128,128]{2,1,0:T(8,128)(2,1)} %get-tuple-element.198, s32[1024]{0:T(1024)S(1)} %pad_clamp_fusion.8), kind=kCustom, calls=%fused_computation.clone.1.clone | custom fusion | bytes 33556480 | tf_op jit(solution)/shard_map/while/body/eval_jaxpr/gather | solution.py:53
  370.5 11.2 %bitcast_dynamic-update-slice_fusion.6 = bf16[2,16,2,128,128]{3,4,2,1,0:T(8,128)(2,1)S(1)} fusion(bf16[2,16,2,128,128]{3,4,2,1,0:T(8,128)(2,1)S(1)} %get-tuple-element.191, s32[]{:T(128)} %get-tuple-element.190, bf16[16,2,16,128,128]{4,3,2,1,0:T(8,128)(2,1)} %bitcast.98, bf16[2,16,16,128,128]{4,3,2,1,0:T(8,128)(2,1)} %get-tuple-element.199), kind=kOutput, calls=%fused_computation.7.clone.1.clone | convolution fusion | flops 2147483648 | bytes 27264000 | tf_op jit(solution)/shard_map/while/body/eval_jaxpr/gtab,gstbc->gsac/dot_general | solution.py:54
  381.9 21.9 %gather_fusion = bf16[512,128,128]{2,1,0:T(8,128)(2,1)} fusion(bf16[769,128,128]{2,1,0:T(8,128)(2,1)} %get-tuple-element.198, s32[1024]{0:T(1024)S(1)} %pad_clamp_fusion.8), kind=kCustom, calls=%fused_computation.clone.1.clone | custom fusion | bytes 33556480 | tf_op jit(solution)/shard_map/while/body/eval_jaxpr/gather | solution.py:53
  403.7 11.2 %bitcast_dynamic-update-slice_fusion.6 = bf16[2,16,2,128,128]{3,4,2,1,0:T(8,128)(2,1)S(1)} fusion(bf16[2,16,2,128,128]{3,4,2,1,0:T(8,128)(2,1)S(1)} %get-tuple-element.191, s32[]{:T(128)} %get-tuple-element.190, bf16[16,2,16,128,128]{4,3,2,1,0:T(8,128)(2,1)} %bitcast.98, bf16[2,16,16,128,128]{4,3,2,1,0:T(8,128)(2,1)} %get-tuple-element.199), kind=kOutput, calls=%fused_computation.7.clone.1.clone | convolution fusion | flops 2147483648 | bytes 27264000 | tf_op jit(solution)/shard_map/while/body/eval_jaxpr/gtab,gstbc->gsac/dot_general | solution.py:54
  417.1 84.1 %all-gather.2.cloned.1.call-done = bf16[32,16,128,128]{2,3,1,0:T(8,128)(2,1)} async-done(((bf16[32,2,128,128]{2,3,1,0:T(8,128)(2,1)}), bf16[32,16,128,128]{2,3,1,0:T(8,128)(2,1)}) %all-gather.2.cloned.1.call-update) | async-done | bytes 16777232 | tf_op jit(solution)/shard_map/all_gather | solution.py:81
  501.1 22.5 %copy.62 = bf16[32,16,128,128]{3,2,1,0:T(8,128)(2,1)} copy(bf16[32,16,128,128]{2,3,1,0:T(8,128)(2,1)} %all-gather.2.cloned.1.call-done) | data formatting | bytes 33554432 | tf_op jit(solution)/shard_map/all_gather | solution.py:81
  523.7 67.6 %while.23 = (s32[]{:T(128)}, f32[2,16,2,128,128]{3,4,2,1,0:T(8,128)}, s32[2,16,2,16]{3,2,1,0:T(2,128)S(1)}, bf16[769,128,128]{2,1,0:T(8,128)(2,1)}, bf16[2,16,16,128,128]{4,3,2,1,0:T(8,128)(2,1)}) while((s32[]{:T(128)}, f32[2,16,2,128,128]{3,4,2,1,0:T(8,128)}, s32[2,16,2,16]{3,2,1,0:T(2,128)S(1)}, ...), condition=%wide.region_5.6_spmd.clone, body=%wide.region_4.5_spmd.sunk.clone | while | flops 2147486208 | bytes 60834880 | solution.py:56
  523.8 22.0 %gather_fusion.1 = bf16[512,128,128]{2,1,0:T(8,128)(2,1)} fusion(bf16[769,128,128]{2,1,0:T(8,128)(2,1)} %get-tuple-element.213, s32[1024]{0:T(1024)S(1)} %pad_clamp_fusion.9), kind=kCustom, calls=%fused_computation.1.clone.1.clone | custom fusion | bytes 33556480 | tf_op jit(solution)/shard_map/while/body/eval_jaxpr/gather | solution.py:53
  545.8 11.7 %bitcast_dynamic-update-slice_fusion.7 = f32[2,16,2,128,128]{3,4,2,1,0:T(8,128)} fusion(f32[2,16,2,128,128]{3,4,2,1,0:T(8,128)} %get-tuple-element.206, s32[]{:T(128)} %get-tuple-element.205, bf16[16,2,16,128,128]{4,3,2,1,0:T(8,128)(2,1)} %bitcast.99, bf16[2,16,16,128,128]{4,3,2,1,0:T(8,128)(2,1)} %get-tuple-element.214), kind=kOutput, calls=%fused_computation.14.clone.1.clone | convolution fusion | flops 2147483648 | bytes 27264000 | tf_op jit(solution)/shard_map/while/body/eval_jaxpr/gtab,gstbc->gsac/dot_general | solution.py:54
  557.6 21.9 %gather_fusion.1 = bf16[512,128,128]{2,1,0:T(8,128)(2,1)} fusion(bf16[769,128,128]{2,1,0:T(8,128)(2,1)} %get-tuple-element.213, s32[1024]{0:T(1024)S(1)} %pad_clamp_fusion.9), kind=kCustom, calls=%fused_computation.1.clone.1.clone | custom fusion | bytes 33556480 | tf_op jit(solution)/shard_map/while/body/eval_jaxpr/gather | solution.py:53
  579.5 11.8 %bitcast_dynamic-update-slice_fusion.7 = f32[2,16,2,128,128]{3,4,2,1,0:T(8,128)} fusion(f32[2,16,2,128,128]{3,4,2,1,0:T(8,128)} %get-tuple-element.206, s32[]{:T(128)} %get-tuple-element.205, bf16[16,2,16,128,128]{4,3,2,1,0:T(8,128)(2,1)} %bitcast.99, bf16[2,16,16,128,128]{4,3,2,1,0:T(8,128)(2,1)} %get-tuple-element.214), kind=kOutput, calls=%fused_computation.14.clone.1.clone | convolution fusion | flops 2147483648 | bytes 27264000 | tf_op jit(solution)/shard_map/while/body/eval_jaxpr/gtab,gstbc->gsac/dot_general | solution.py:54
  591.2 2.9 subtract_convert_fusion
  594.4 2.7 gather_fusion.3
  597.1 3.5 copy.65
  600.6 47.1 %all_to_all.11 = bf16[16,6,128,128]{3,2,1,0:T(8,128)(2,1)S(1)} all-to-all(bf16[16,6,128,128]{3,2,1,0:T(8,128)(2,1)S(1)} %bitcast.106), channel_id=1, replica_groups=mesh['row'=16,'col'=8] {'row'}, dimensions={0} | all-to-all | bytes 6291456 | tf_op jit(solution)/shard_map/all_to_all | solution.py:105
  (56 shorter events, 11.1 us)
Async XLA Ops:
  6.5 494.6 %all-gather.2.cloned.1.call-start = ((), (), s32[]{:S(2)}) async-start(), calls=%async_computation.2 | async-start | bytes 18874368 | tf_op jit(solution)/shard_map/all_gather | solution.py:81
  203.9 8.2 %copy-start = (bf16[8,32,2,128,128]{4,3,2,0,1:T(8,128)(2,1)}, bf16[8,32,2,128,128]{4,3,2,0,1:T(8,128)(2,1)S(1)}, u32[]{:S(2)}) copy-start(bf16[8,32,2,128,128]{4,3,2,0,1:T(8,128)(2,1)S(1)} %copy.76) | copy-start | bytes 50331652
  203.9 14.4 %copy-start.3 = (s32[512,16]{0,1:T(8,128)S(1)}, s32[512,16]{0,1:T(8,128)}, u32[]{:S(2)}) copy-start(s32[512,16]{0,1:T(8,128)} %param.8) | copy-start | bytes 98308
  212.1 96.8 %collective-permute-start = (bf16[8,16,128,128]{3,2,1,0:T(8,128)(2,1)}, bf16[8,16,128,128]{3,2,1,0:T(8,128)(2,1)}, u32[]{:S(2)}, u32[]{:S(2)}) collective-permute-start(bf16[8,16,128,128]{3,2,1,0:T(8,128)(2,1)} %bitcast.23), channel_id=1, source_target_pairs={{0,8},{8,16},{16,24},{24,32},{32,40},{40,48},{48,56},{56,64},{64,7... | collective-permute-start | bytes 12582920 | tf_op jit(solution)/shard_map/ppermute | solution.py:15
  214.1 94.8 %collective-permute-start.1 = (bf16[8,16,128,128]{3,2,1,0:T(8,128)(2,1)}, bf16[8,16,128,128]{3,2,1,0:T(8,128)(2,1)}, u32[]{:S(2)}, u32[]{:S(2)}) collective-permute-start(bf16[8,16,128,128]{3,2,1,0:T(8,128)(2,1)} %bitcast.25), channel_id=1, source_target_pairs={{8,0},{16,8},{24,16},{32,24},{40,32},{48,40},{56,48},{64,56},{72,6... | collective-permute-start | bytes 12582920 | tf_op jit(solution)/shard_map/ppermute | solution.py:16
  348.6 67.7 %copy-start.4 = (s32[1,32,2,1]{1,3,2,0:T(1,128)S(1)}, s32[1,32,2,1]{1,3,2,0:T(1,128)}, u32[]{:S(2)}) copy-start(s32[1,32,2,1]{1,3,2,0:T(1,128)} %param.9) | copy-start | bytes 772
  414.9 1.3 copy-start.1
  523.7 67.6 %copy-start.2 = (bf16[2,16,2,128,128]{3,4,2,1,0:T(8,128)(2,1)S(1)}, bf16[2,16,2,128,128]{3,4,2,1,0:T(8,128)(2,1)}, u32[]{:S(2)}) copy-start(bf16[2,16,2,128,128]{3,4,2,1,0:T(8,128)(2,1)} %copy-done.1) | copy-start | bytes 6291460
Sparse Core Ops, SparseCore 0:
  416.4 84.6 all-gather.1
